TPU v7x, 32 devices: a whole 2x2x4 slice. The times are simulated.
32 devices in a mesh: pb: 4 (over z), row: 4 (over y, x), col: 2 (over core).
Axes of the slice: x: 2, y: 2, z: 4, core: 2. Of those that a mesh axis runs over, the one named last changes fastest.
Arguments:
- amplitudes: bfloat16 [4, 20, 4, 9216], P('pb'), may hold values from -6 to 6
- pairs: int32 [4, 4, 2], P('pb'), may hold values from 0 to 3
- stored_k: int32 [4], replicated, may hold values from 0 to 3, each once
- orbitals: bfloat16 [4, 192, 2048], P('pb', None, ('row', 'col')), may hold values from -1.078125 to 1.078125
- valence_energy: float32 [4, 96], replicated, may hold values from -1 to 0
- conduction_energy: float32 [4, 96], replicated, may hold values from 2.5 to 3.5
- screened: bfloat16 [4, 2048, 2048], P('pb', 'row', 'col'), may hold values from -0.125 to 0.125
Outputs:
- filtered: bfloat16 [4, 20, 4, 9216], P('pb')
Inputs may be any that keep to these rules, and one draw needn't show every extreme that they name: stored_k holds every k-point exactly once; row s of orbitals belongs to k-point stored_k[s]. `pairs`: each entry is a k-point.
All inputs are finite; a program needn't handle non-finite values.
Results may differ from a plain program's by a relative error of at most 0.024.
Values may be sent and summed in bfloat16 or wider, within the bound.
A program may use at most 64 MiB of HBM per device.

v0:
```python
import jax
import jax.numpy as jnp
from jax import lax
from jax.sharding import PartitionSpec as P

CENTER = 3.0
HALF = 2.5


def on_device(amplitudes, pairs, stored_k, orbitals, valence_energy, conduction_energy, screened):
    amplitude = amplitudes[0]
    pair_list = pairs[0]
    w_tile = screened[0]
    count_v = valence_energy.shape[1]
    count_c = conduction_energy.shape[1]
    vectors, pair_count, flat_size = amplitude.shape
    points = orbitals.shape[2]
    col_width = w_tile.shape[1]
    column = lax.axis_index("col")

    def pick(shard_piece):
        pick_low = (stored_k[None, :] == pair_list[:, 0:1]).astype(jnp.bfloat16)
        pick_high = (stored_k[None, :] == pair_list[:, 1:2]).astype(jnp.bfloat16)
        low_bands = jnp.einsum(
            "pl,lbr->pbr", pick_low, shard_piece[:, :count_v], preferred_element_type=jnp.float32
        )
        high_bands = jnp.einsum(
            "pl,lbr->pbr", pick_high, shard_piece[:, count_v:], preferred_element_type=jnp.float32
        )
        return (low_bands, high_bands)

    def fetch_each():
        found = pick(lax.all_gather(orbitals, "pb", axis=0, tiled=True))
        return (found[0].astype(jnp.bfloat16), found[1].astype(jnp.bfloat16))

    low_energy = jnp.take(valence_energy, pair_list[:, 0], axis=0)
    high_energy = jnp.take(conduction_energy, pair_list[:, 1], axis=0)
    gap_grid = (high_energy[:, None, :] - low_energy[:, :, None]).reshape(pair_count, flat_size)
    gap_rows = jnp.tile(gap_grid, (vectors, 1))

    def kernel_term(current, bands):
        valence, conduction_orbital = bands
        amplitude_lattice = current.reshape(vectors, pair_count, count_v, count_c)
        inner_total_sum = jnp.einsum(
            "iomx,oxj->iomj",
            amplitude_lattice,
            conduction_orbital,
            preferred_element_type=jnp.float32,
        )
        values = jnp.sum(valence.astype(jnp.float32)[None] * inner_total_sum, axis=2)
        values = values.astype(jnp.bfloat16).reshape(vectors * pair_count, points)
        everywhere = lax.all_gather(values, ("row", "col"), axis=1, tiled=True)
        needed = lax.dynamic_slice_in_dim(everywhere, column * col_width, col_width, 1)
        partial_value = lax.dot_general(
            needed, w_tile, (((1,), (1,)), ((), ())), preferred_element_type=jnp.float32
        )
        own_sums = (
            lax.psum_scatter(
                partial_value.astype(jnp.bfloat16), "col", scatter_dimension=1, tiled=True
            )
            .astype(jnp.float32)
            .reshape(vectors, pair_count, points)
        )
        weighted_product = (valence.astype(jnp.float32)[None] * own_sums[:, :, None, :]).astype(
            jnp.bfloat16
        )
        projected = jnp.einsum(
            "kyqz,yhz->kyqh",
            weighted_product,
            conduction_orbital,
            preferred_element_type=jnp.float32,
        )
        return projected.reshape(vectors * pair_count, flat_size)

    def advance(current_rows, summed, gap_part, previous_rows, factor):
        value = (gap_part * current_rows + summed - CENTER * current_rows) / HALF
        if previous_rows is None:
            return value.astype(jnp.bfloat16)
        return (factor * value - previous_rows).astype(jnp.bfloat16)

    def finish(partial_term, current, previous, factor):
        summed = lax.psum(partial_term.astype(jnp.bfloat16), ("row", "col")).astype(jnp.float32)
        previous_full = None
        if previous is not None:
            previous_full = previous.astype(jnp.float32)
        return advance(current.astype(jnp.float32), summed, gap_rows, previous_full, factor)

    initial = amplitude.reshape(vectors * pair_count, flat_size)
    first_bands = fetch_each()
    first_term = finish(kernel_term(initial, first_bands), initial, None, 1.0)
    second_bands = fetch_each()
    second_term = finish(kernel_term(first_term, second_bands), first_term, initial, 2.0)
    return second_term.reshape(1, vectors, pair_count, flat_size)


def solution(mesh):
    return jax.shard_map(
        on_device,
        mesh=mesh,
        in_specs=(
            P("pb", None, None, None),
            P("pb", None, None),
            P(),
            P("pb", None, ("row", "col")),
            P(),
            P(),
            P("pb", "row", "col"),
        ),
        out_specs=P("pb", None, None, None),
        check_vma=False,
    )
```

profile of v0, /device:TPU:0, one launch (start us, length us, event | category | flops | bytes accessed | tf_op | source)
XLA Modules:
  0.0 231.6 jit_solution(977043757335007725)
XLA Ops:
  6.5 0.0 copy-start
  6.5 0.0 copy-start.1
  6.5 0.0 reduce-scatter.3.cloned.1.call-start
  6.5 0.8 slice_bitcast_fusion.1
  7.4 0.0 copy-start.5
  7.4 16.6 %all_gather.10 = bf16[4,192,256]{2,1,0:T(8,128)(2,1)S(1)} all-gather(bf16[1,192,256]{2,1,0:T(8,128)(2,1)} %param.12), channel_id=1, replica_groups=mesh['pb'=4,'row'=4,'col'=2] {'pb'}, dimensions={0}, use_global_device_ids=true | all-gather | bytes 491520 | tf_op jit(solution)/shard_map/all_gather | solution.py:33
  24.0 1.0 fusion.15
  25.0 0.1 copy.59
  25.1 0.0 copy-done.1
  25.1 2.6 %reshape_reshape_squeeze.3 = bf16[20,4,96,96]{3,2,1,0:T(8,128)(2,1)} reshape(bf16[1,20,4,9216]{3,2,1,0:T(4,128)(2,1)S(1)} %copy-done.1) | data formatting | bytes 2949120 | tf_op jit(solution)/shard_map/reshape;reshape;squeeze | solution.py:43
  27.7 0.0 copy-done.5
  27.7 0.3 fusion.16
  28.0 0.0 copy-start.6
  28.0 2.8 %fusion.1 = bf16[20,4,256]{2,0,1:T(8,128)(2,1)S(1)} fusion(f32[4,96,256]{2,1,0:T(8,128)S(1)} %copy.59, bf16[20,4,96,96]{3,2,1,0:T(8,128)(2,1)} %reshape_reshape_squeeze.3, bf16[4,96,256,1]{2,0,1,3:T(4,128)(2,1)S(1)} %fusion.16), kind=kOutput, calls=%fused_computation.5 | convolution fusion | flops 381399040 | bytes 2105344 | tf_op jit(solution)/shard_map/iomx,oxj->iomj/dot_general | solution.py:44
  30.8 0.0 copy-done.6
  30.9 10.1 %all_gather.11 = bf16[80,2048]{1,0:T(8,128)(2,1)S(1)} all-gather(bf16[80,256]{1,0:T(8,128)(2,1)S(1)} %convert_element_type.92), channel_id=1, replica_groups=mesh['pb'=4,'row'=4,'col'=2] {'row','col'}, dimensions={1}, use_global_device_ids=true | all-gather | bytes 368640 | tf_op jit(solution)/shard_map/all_gather | solution.py:52
  41.0 0.0 copy-start.4
  41.0 0.0 copy-done
  41.0 1.1 convolution_convert_fusion.3
  42.1 0.0 copy-start.7
  42.1 0.0 reduce-scatter.3.cloned.1.call-update
  42.1 0.0 all-reduce.3.cloned.1.call-start
  42.2 1.7 reshape.48
  43.9 0.0 copy-done.4
  43.9 6.7 %reduce-scatter.3.cloned.1.call-done = bf16[80,256]{1,0:T(8,128)(2,1)} async-done(((bf16[80,512]{1,0:T(8,128)(2,1)}), bf16[80,256]{1,0:T(8,128)(2,1)}) %reduce-scatter.3.cloned.1.call-update) | async-done | bytes 40976 | tf_op jit(solution)/shard_map/reduce_scatter | solution.py:58
  50.6 0.8 reshape.49
  51.4 0.0 copy-done.7
  51.4 2.9 %convert_bitcast_fusion.1 = bf16[20,4,96,96]{2,3,0,1:T(8,128)(2,1)} fusion(f32[20,4,256]{2,0,1:T(8,128)S(1)} %copy.63, f32[4,96,256]{2,1,0:T(8,128)S(1)} %copy.59, bf16[4,96,256,1]{2,0,1,3:T(4,128)(2,1)S(1)} %copy-done.7), kind=kOutput, calls=%fused_computation.25 | convolution fusion | flops 382156800 | bytes 2146304 | tf_op jit(solution)/shard_map/kyqz,yhz->kyqh/dot_general | solution.py:67
  54.3 3.2 %copy.65 = bf16[20,4,96,96]{3,2,1,0:T(8,128)(2,1)S(1)} copy(bf16[20,4,96,96]{2,3,0,1:T(8,128)(2,1)} %convert_bitcast_fusion.1) | data formatting | bytes 2949120 | tf_op jit(solution)/shard_map/convert_element_type | solution.py:82
  57.5 0.0 copy-start.2
  57.5 0.0 copy-start.3
  57.6 3.6 %convert_element_type.97 = bf16[80,9216]{1,0:T(8,128)(2,1)} reshape(bf16[20,4,96,96]{3,2,1,0:T(8,128)(2,1)S(1)} %copy.65) | data formatting | bytes 2949120 | tf_op jit(solution)/shard_map/convert_element_type | solution.py:82
  61.1 0.0 all-reduce.3.cloned.1.call-update
  61.1 0.0 reduce-scatter.5.cloned.1.call-start
  61.2 0.0 copy-done.2
  61.2 0.6 gather_fusion.1
  61.8 0.0 copy-done.3
  61.8 0.6 gather_fusion
  62.3 0.1 broadcast_select_fusion
  62.4 0.1 broadcast_select_fusion.1
  62.5 0.1 broadcast_subtract_fusion
  62.6 0.2 sub.32
  62.8 2.3 tile.8
  65.0 4.3 %tile.9 = f32[80,9216]{1,0:T(8,128)} reshape(f32[20,4,9216]{2,1,0:T(4,128)} %tile.8) | data formatting | bytes 5898240 | tf_op jit(solution)/shard_map/tile | solution.py:39
  69.3 51.5 %all-reduce.3.cloned.1.call-done = bf16[80,9216]{1,0:T(8,128)(2,1)} async-done(((bf16[80,9216]{1,0:T(8,128)(2,1)}), bf16[80,9216]{1,0:T(8,128)(2,1)}) %all-reduce.3.cloned.1.call-update) | async-done | bytes 1474576 | tf_op jit(solution)/shard_map/psum | solution.py:82
  120.8 3.8 %multiply_convert_fusion.4 = bf16[80,9216]{1,0:T(8,128)(2,1)S(1)} fusion(f32[80,9216]{1,0:T(8,128)} %reshape.48, bf16[80,9216]{1,0:T(8,128)(2,1)} %all-reduce.3.cloned.1.call-done, f32[80,9216]{1,0:T(8,128)} %tile.9), kind=kLoop, calls=%fused_computation.21 | loop fusion | flops 5160960 | bytes 8847360 | tf_op jit(solution)/shard_map/convert_element_type | solution.py:78
  124.6 0.0 copy-start.8
  124.6 2.9 %reshape.46 = bf16[20,4,96,96]{3,2,1,0:T(8,128)(2,1)} reshape(bf16[80,9216]{1,0:T(8,128)(2,1)S(1)} %multiply_convert_fusion.4) | data formatting | bytes 2949120 | tf_op jit(solution)/shard_map/reshape | solution.py:43
  127.6 0.0 copy-done.8
  127.6 2.7 %fusion = bf16[20,4,256]{2,0,1:T(8,128)(2,1)S(1)} fusion(f32[4,96,256]{2,1,0:T(8,128)S(1)} %copy.59, bf16[20,4,96,96]{3,2,1,0:T(8,128)(2,1)} %reshape.46, bf16[4,96,256,1]{2,0,1,3:T(4,128)(2,1)S(1)} %copy-done.8), kind=kOutput, calls=%fused_computation.3 | convolution fusion | flops 381399040 | bytes 2105344 | tf_op jit(solution)/shard_map/iomx,oxj->iomj/dot_general | solution.py:44
  130.4 9.5 %all_gather.12 = bf16[80,2048]{1,0:T(8,128)(2,1)S(1)} all-gather(bf16[80,256]{1,0:T(8,128)(2,1)S(1)} %convert_element_type.102), channel_id=1, replica_groups=mesh['pb'=4,'row'=4,'col'=2] {'row','col'}, dimensions={1}, use_global_device_ids=true | all-gather | bytes 368640 | tf_op jit(solution)/shard_map/all_gather | solution.py:52
  139.8 1.1 convolution_convert_fusion.2
  140.9 0.0 reduce-scatter.5.cloned.1.call-update
  140.9 0.2 all-reduce.5.cloned.1.call-start
  141.2 7.4 %reduce-scatter.5.cloned.1.call-done = bf16[80,256]{1,0:T(8,128)(2,1)} async-done(((bf16[80,512]{1,0:T(8,128)(2,1)}), bf16[80,256]{1,0:T(8,128)(2,1)}) %reduce-scatter.5.cloned.1.call-update) | async-done | bytes 40976 | tf_op jit(solution)/shard_map/reduce_scatter | solution.py:58
  148.6 0.8 reshape.50
  149.4 2.9 %convert_bitcast_fusion = bf16[20,4,96,96]{2,3,0,1:T(8,128)(2,1)} fusion(f32[20,4,256]{2,0,1:T(8,128)S(1)} %copy.69, f32[4,96,256]{2,1,0:T(8,128)S(1)} %copy.59, bf16[4,96,256,1]{2,0,1,3:T(4,128)(2,1)S(1)} %copy-done.8), kind=kOutput, calls=%fused_computation.24 | convolution fusion | flops 382156800 | bytes 2146304 | tf_op jit(solution)/shard_map/kyqz,yhz->kyqh/dot_general | solution.py:67
  152.3 3.2 %copy.71 = bf16[20,4,96,96]{3,2,1,0:T(8,128)(2,1)S(1)} copy(bf16[20,4,96,96]{2,3,0,1:T(8,128)(2,1)} %convert_bitcast_fusion) | data formatting | bytes 2949120 | tf_op jit(solution)/shard_map/convert_element_type | solution.py:82
  155.5 3.6 %convert_element_type.107 = bf16[80,9216]{1,0:T(8,128)(2,1)} reshape(bf16[20,4,96,96]{3,2,1,0:T(8,128)(2,1)S(1)} %copy.71) | data formatting | bytes 2949120 | tf_op jit(solution)/shard_map/convert_element_type | solution.py:82
  159.1 0.0 all-reduce.5.cloned.1.call-update
  159.1 59.7 %all-reduce.5.cloned.1.call-done = bf16[80,9216]{1,0:T(8,128)(2,1)} async-done(((bf16[80,9216]{1,0:T(8,128)(2,1)}), bf16[80,9216]{1,0:T(8,128)(2,1)}) %all-reduce.5.cloned.1.call-update) | async-done | bytes 1474576 | tf_op jit(solution)/shard_map/psum | solution.py:82
  218.8 4.8 %fusion.12 = bf16[80,9216]{1,0:T(8,128)(2,1)S(1)} fusion(f32[80,9216]{1,0:T(8,128)} %reshape.48, f32[80,9216]{1,0:T(8,128)} %tile.9, bf16[80,9216]{1,0:T(8,128)(2,1)} %all-reduce.5.cloned.1.call-done, bf16[80,9216]{1,0:T(8,128)(2,1)} %all-reduce.3.cloned.1.call-done), kind=kLoop, calls=%fused_computation.20 | loop fusion | flops 11796480 | bytes 10321920 | tf_op jit(solution)/shard_map/convert_element_type | solution.py:79
  223.6 1.4 reshape.47
  (9 shorter events, 0.1 us)
Async XLA Ops:
  6.5 34.5 %copy-start = (bf16[1,512,1024]{2,1,0:T(8,128)(2,1)S(1)}, bf16[1,512,1024]{2,1,0:T(8,128)(2,1)}, u32[]{:S(2)}) copy-start(bf16[1,512,1024]{2,1,0:T(8,128)(2,1)} %param.15) | copy-start | bytes 3145732
  6.5 18.5 %copy-start.1 = (bf16[1,20,4,9216]{3,2,1,0:T(4,128)(2,1)S(1)}, bf16[1,20,4,9216]{3,2,1,0:T(4,128)(2,1)}, u32[]{:S(2)}) copy-start(bf16[1,20,4,9216]{3,2,1,0:T(4,128)(2,1)} %param.9) | copy-start | bytes 4423684
  6.5 44.1 %reduce-scatter.3.cloned.1.call-start = ((), (), s32[]{:S(2)}) async-start(), calls=%async_computation.2 | async-start | bytes 122880 | tf_op jit(solution)/shard_map/reduce_scatter | solution.py:58
  7.4 20.3 %copy-start.5 = (s32[4]{0:T(128)S(1)}, s32[4]{0:T(128)}, u32[]{:S(2)}) copy-start(s32[4]{0:T(128)} %param.11) | copy-start | bytes 52
  28.0 2.8 %copy-start.6 = (bf16[4,96,256,1]{2,0,1,3:T(4,128)(2,1)}, bf16[4,96,256,1]{2,0,1,3:T(4,128)(2,1)S(1)}, u32[]{:S(2)}) copy-start(bf16[4,96,256,1]{2,0,1,3:T(4,128)(2,1)S(1)} %fusion.16) | copy-start | bytes 589828
  41.0 2.9 %copy-start.4 = (s32[1,4,2]{1,2,0:T(2,128)S(1)}, s32[1,4,2]{1,2,0:T(2,128)}, u32[]{:S(2)}) copy-start(s32[1,4,2]{1,2,0:T(2,128)} %param.10) | copy-start | bytes 100
  42.1 9.3 %copy-start.7 = (bf16[4,96,256,1]{2,0,1,3:T(4,128)(2,1)S(1)}, bf16[4,96,256,1]{2,0,1,3:T(4,128)(2,1)}, u32[]{:S(2)}) copy-start(bf16[4,96,256,1]{2,0,1,3:T(4,128)(2,1)} %copy-done.6) | copy-start | bytes 589828
  42.1 78.7 %all-reduce.3.cloned.1.call-start = ((), (), s32[]{:S(2)}) async-start(), calls=%async_computation.3 | async-start | bytes 2949120 | tf_op jit(solution)/shard_map/psum | solution.py:82
  57.5 3.7 %copy-start.2 = (f32[4,96]{1,0:T(4,128)S(1)}, f32[4,96]{1,0:T(4,128)}, u32[]{:S(2)}) copy-start(f32[4,96]{1,0:T(4,128)} %param.13) | copy-start | bytes 4612
  57.5 4.2 %copy-start.3 = (f32[4,96]{1,0:T(4,128)S(1)}, f32[4,96]{1,0:T(4,128)}, u32[]{:S(2)}) copy-start(f32[4,96]{1,0:T(4,128)} %param.14) | copy-start | bytes 4612
  61.1 87.5 %reduce-scatter.5.cloned.1.call-start = ((), (), s32[]{:S(2)}) async-start(), calls=%async_computation.4 | async-start | bytes 122880 | tf_op jit(solution)/shard_map/reduce_scatter | solution.py:58
  124.6 2.9 %copy-start.8 = (bf16[4,96,256,1]{2,0,1,3:T(4,128)(2,1)S(1)}, bf16[4,96,256,1]{2,0,1,3:T(4,128)(2,1)}, u32[]{:S(2)}) copy-start(bf16[4,96,256,1]{2,0,1,3:T(4,128)(2,1)} %copy-done.6) | copy-start | bytes 589828
  140.9 77.9 %all-reduce.5.cloned.1.call-start = ((), (), s32[]{:S(2)}) async-start(), calls=%async_computation.5 | async-start | bytes 2949120 | tf_op jit(solution)/shard_map/psum | solution.py:82
Sparse Core Ops, SparseCore 0:
  42.2 8.3 reduce-scatter.2
  61.3 59.5 all-reduce.2
  141.1 7.5 reduce-scatter.4
  159.2 59.5 all-reduce.4
where the time goes:
time: 232 us
  waiting for transfers between devices  125 us (54%)
  blocking collectives  36.2 us (16%)
  local copies, waits for them, and re-layouts  32.7 us (14%)
  matrix products  14.8 us (6%)
  between operations  13.3 us (6%)
  other arithmetic  8.91 us (4%)
    psum x2, waiting for transfers between devices, finish(): lax.psum(partial_term.astype(jnp.bfloat16), ('row', 'col'))  111 us
    all_gather x2, blocking collectives, kernel_term(): everywhere = lax.all_gather(values, ('row', 'col'), axis=1, tiled=True)  19.6 us
    all_gather x1, blocking collectives, fetch_each(): found = pick(lax.all_gather(orbitals, 'pb', axis=0, tiled=True))  16.6 us
    reduce_scatter x2, waiting for transfers between devices, kernel_term(): lax.psum_scatter(partial_value.astype(jnp.bfloat16), 'col', scatter_dimen...  14.1 us
    convert_element_type x4, local copies, waits for them, and re-layouts, finish(): partial_term.astype(jnp.bfloat16)  13.5 us
    another operation x2, local copies, waits for them, and re-layouts, on_device(): gap_rows = jnp.tile(gap_grid, (vectors, 1))  6.56 us
    dot_general x2, matrix products, kernel_term(): jnp.einsum('kyqz,yhz->kyqh', weighted_product, conduction_orbital, prefer...  5.75 us
    dot_general x2, matrix products, kernel_term(): jnp.einsum('iomx,oxj->iomj', amplitude_lattice, conduction_orbital, prefe...  5.54 us
  transfers between devices with their start and end apart: 4, of which 4 were waited for; matrix products, arithmetic and copies ran while one was open for 4% of the time, Pallas kernels for 0%

commit v1 on v0

--- a/solution.py
+++ b/solution.py
@@ -49,7 +49,7 @@
         )
         values = jnp.sum(valence.astype(jnp.float32)[None] * inner_total_sum, axis=2)
         values = values.astype(jnp.bfloat16).reshape(vectors * pair_count, points)
-        everywhere = lax.all_gather(values, ("row", "col"), axis=1, tiled=True)
+        everywhere = jnp.concatenate(lax.all_gather(values, ("row", "col")), axis=1)
         needed = lax.dynamic_slice_in_dim(everywhere, column * col_width, col_width, 1)
         partial_value = lax.dot_general(
             needed, w_tile, (((1,), (1,)), ((), ())), preferred_element_type=jnp.float32

time: 232 us -> 231 us (level)
  no operation moved by 1% of the time
where the time goes in v1:
time: 231 us; the launch traced here: 230 us
  waiting for transfers between devices  126 us (55%)
  blocking collectives  35 us (15%)
  local copies, waits for them, and re-layouts  32.7 us (14%)
  matrix products  14.8 us (6%)
  between operations  13.4 us (6%)
  other arithmetic  8.91 us (4%)
    psum x2, waiting for transfers between devices, finish(): lax.psum(partial_term.astype(jnp.bfloat16), ('row', 'col'))  111 us
    all_gather x2, blocking collectives, kernel_term(): everywhere = jnp.concatenate(lax.all_gather(values, ('row', 'col')), axis=1)  18.4 us
    all_gather x1, blocking collectives, fetch_each(): found = pick(lax.all_gather(orbitals, 'pb', axis=0, tiled=True))  16.6 us
    reduce_scatter x2, waiting for transfers between devices, kernel_term(): lax.psum_scatter(partial_value.astype(jnp.bfloat16), 'col', scatter_dimen...  14.4 us
    convert_element_type x4, local copies, waits for them, and re-layouts, finish(): partial_term.astype(jnp.bfloat16)  13.5 us
    another operation x2, local copies, waits for them, and re-layouts, on_device(): gap_rows = jnp.tile(gap_grid, (vectors, 1))  6.53 us
    dot_general x2, matrix products, kernel_term(): jnp.einsum('kyqz,yhz->kyqh', weighted_product, conduction_orbital, prefer...  5.75 us
    dot_general x2, matrix products, kernel_term(): jnp.einsum('iomx,oxj->iomj', amplitude_lattice, conduction_orbital, prefe...  5.54 us
  transfers between devices with their start and end apart: 4, of which 4 were waited for; matrix products, arithmetic and copies ran while one was open for 4% of the time, Pallas kernels for 0%

profile of v1, /device:TPU:0, one launch (start us, length us, event | category | flops | bytes accessed | tf_op | source)
XLA Modules:
  0.0 230.5 jit_solution(8881768181742684789)
XLA Ops:
  6.5 0.0 copy-start
  6.5 0.0 copy-start.1
  6.5 0.0 reduce-scatter.3.cloned.1.call-start
  6.5 0.8 slice_bitcast_fusion.1
  7.4 0.0 copy-start.5
  7.4 16.6 %all_gather.10 = bf16[4,192,256]{2,1,0:T(8,128)(2,1)S(1)} all-gather(bf16[1,192,256]{2,1,0:T(8,128)(2,1)} %param.12), channel_id=1, replica_groups=mesh['pb'=4,'row'=4,'col'=2] {'pb'}, dimensions={0}, use_global_device_ids=true | all-gather | bytes 491520 | tf_op jit(solution)/shard_map/all_gather | solution.py:33
  24.0 1.0 fusion.15
  25.0 0.1 copy.62
  25.1 0.0 copy-done.1
  25.1 2.6 %reshape_reshape_squeeze.3 = bf16[20,4,96,96]{3,2,1,0:T(8,128)(2,1)} reshape(bf16[1,20,4,9216]{3,2,1,0:T(4,128)(2,1)S(1)} %copy-done.1) | data formatting | bytes 2949120 | tf_op jit(solution)/shard_map/reshape;reshape;squeeze | solution.py:43
  27.7 0.0 copy-done.5
  27.7 0.3 fusion.16
  28.0 0.0 copy-start.6
  28.0 2.8 %fusion.1 = bf16[20,4,256]{2,0,1:T(8,128)(2,1)S(1)} fusion(f32[4,96,256]{2,1,0:T(8,128)S(1)} %copy.62, bf16[20,4,96,96]{3,2,1,0:T(8,128)(2,1)} %reshape_reshape_squeeze.3, bf16[4,96,256,1]{2,0,1,3:T(4,128)(2,1)S(1)} %fusion.16), kind=kOutput, calls=%fused_computation.5 | convolution fusion | flops 381399040 | bytes 2105344 | tf_op jit(solution)/shard_map/iomx,oxj->iomj/dot_general | solution.py:44
  30.8 0.0 copy-done.6
  30.9 9.4 %all_gather.11 = bf16[8,80,256]{2,1,0:T(8,128)(2,1)S(1)} all-gather(bf16[1,80,256]{2,1,0:T(8,128)(2,1)S(1)} %convert_element_type.104), channel_id=1, replica_groups=mesh['pb'=4,'row'=4,'col'=2] {'row','col'}, dimensions={0}, use_global_device_ids=true | all-gather | bytes 368640 | tf_op jit(solution)/shard_map/all_gather | solution.py:52
  40.3 0.0 copy-start.4
  40.4 0.0 copy-done
  40.4 1.1 convolution_convert_fusion.3
  41.5 0.0 copy-start.7
  41.5 0.0 reduce-scatter.3.cloned.1.call-update
  41.5 0.0 all-reduce.3.cloned.1.call-start
  41.5 1.7 reshape.80
  43.3 0.0 copy-done.4
  43.3 6.7 %reduce-scatter.3.cloned.1.call-done = bf16[80,256]{1,0:T(8,128)(2,1)} async-done(((bf16[80,512]{1,0:T(8,128)(2,1)}), bf16[80,256]{1,0:T(8,128)(2,1)}) %reduce-scatter.3.cloned.1.call-update) | async-done | bytes 40976 | tf_op jit(solution)/shard_map/reduce_scatter | solution.py:58
  50.0 0.8 reshape.81
  50.8 0.0 copy-done.7
  50.8 2.9 %convert_bitcast_fusion.1 = bf16[20,4,96,96]{2,3,0,1:T(8,128)(2,1)} fusion(f32[20,4,256]{2,0,1:T(8,128)S(1)} %copy.67, f32[4,96,256]{2,1,0:T(8,128)S(1)} %copy.62, bf16[4,96,256,1]{2,0,1,3:T(4,128)(2,1)S(1)} %copy-done.7), kind=kOutput, calls=%fused_computation.25 | convolution fusion | flops 382156800 | bytes 2146304 | tf_op jit(solution)/shard_map/kyqz,yhz->kyqh/dot_general | solution.py:67
  53.7 3.2 %copy.69 = bf16[20,4,96,96]{3,2,1,0:T(8,128)(2,1)S(1)} copy(bf16[20,4,96,96]{2,3,0,1:T(8,128)(2,1)} %convert_bitcast_fusion.1) | data formatting | bytes 2949120 | tf_op jit(solution)/shard_map/convert_element_type | solution.py:82
  56.9 0.0 copy-start.2
  56.9 0.0 copy-start.3
  57.0 3.6 %convert_element_type.109 = bf16[80,9216]{1,0:T(8,128)(2,1)} reshape(bf16[20,4,96,96]{3,2,1,0:T(8,128)(2,1)S(1)} %copy.69) | data formatting | bytes 2949120 | tf_op jit(solution)/shard_map/convert_element_type | solution.py:82
  60.5 0.0 all-reduce.3.cloned.1.call-update
  60.5 0.0 reduce-scatter.5.cloned.1.call-start
  60.6 0.0 copy-done.2
  60.6 0.6 gather_fusion.1
  61.2 0.0 copy-done.3
  61.2 0.6 gather_fusion
  61.7 0.1 broadcast_select_fusion
  61.8 0.1 broadcast_select_fusion.1
  61.9 0.1 broadcast_subtract_fusion
  62.0 0.2 sub.32
  62.2 2.3 tile.8
  64.4 4.3 %tile.9 = f32[80,9216]{1,0:T(8,128)} reshape(f32[20,4,9216]{2,1,0:T(4,128)} %tile.8) | data formatting | bytes 5898240 | tf_op jit(solution)/shard_map/tile | solution.py:39
  68.7 51.5 %all-reduce.3.cloned.1.call-done = bf16[80,9216]{1,0:T(8,128)(2,1)} async-done(((bf16[80,9216]{1,0:T(8,128)(2,1)}), bf16[80,9216]{1,0:T(8,128)(2,1)}) %all-reduce.3.cloned.1.call-update) | async-done | bytes 1474576 | tf_op jit(solution)/shard_map/psum | solution.py:82
  120.2 3.8 %multiply_convert_fusion.4 = bf16[80,9216]{1,0:T(8,128)(2,1)S(1)} fusion(f32[80,9216]{1,0:T(8,128)} %reshape.80, bf16[80,9216]{1,0:T(8,128)(2,1)} %all-reduce.3.cloned.1.call-done, f32[80,9216]{1,0:T(8,128)} %tile.9), kind=kLoop, calls=%fused_computation.21 | loop fusion | flops 5160960 | bytes 8847360 | tf_op jit(solution)/shard_map/convert_element_type | solution.py:78
  124.0 0.0 copy-start.8
  124.0 2.9 %reshape.76 = bf16[20,4,96,96]{3,2,1,0:T(8,128)(2,1)} reshape(bf16[80,9216]{1,0:T(8,128)(2,1)S(1)} %multiply_convert_fusion.4) | data formatting | bytes 2949120 | tf_op jit(solution)/shard_map/reshape | solution.py:43
  126.9 0.0 copy-done.8
  126.9 2.7 %fusion = bf16[20,4,256]{2,0,1:T(8,128)(2,1)S(1)} fusion(f32[4,96,256]{2,1,0:T(8,128)S(1)} %copy.62, bf16[20,4,96,96]{3,2,1,0:T(8,128)(2,1)} %reshape.76, bf16[4,96,256,1]{2,0,1,3:T(4,128)(2,1)S(1)} %copy-done.8), kind=kOutput, calls=%fused_computation.3 | convolution fusion | flops 381399040 | bytes 2105344 | tf_op jit(solution)/shard_map/iomx,oxj->iomj/dot_general | solution.py:44
  129.7 9.0 %all_gather.12 = bf16[8,80,256]{2,1,0:T(8,128)(2,1)S(1)} all-gather(bf16[1,80,256]{2,1,0:T(8,128)(2,1)S(1)} %convert_element_type.114), channel_id=1, replica_groups=mesh['pb'=4,'row'=4,'col'=2] {'row','col'}, dimensions={0}, use_global_device_ids=true | all-gather | bytes 368640 | tf_op jit(solution)/shard_map/all_gather | solution.py:52
  138.7 1.1 convolution_convert_fusion.2
  139.8 0.0 reduce-scatter.5.cloned.1.call-update
  139.8 0.0 all-reduce.5.cloned.1.call-start
  139.9 7.6 %reduce-scatter.5.cloned.1.call-done = bf16[80,256]{1,0:T(8,128)(2,1)} async-done(((bf16[80,512]{1,0:T(8,128)(2,1)}), bf16[80,256]{1,0:T(8,128)(2,1)}) %reduce-scatter.5.cloned.1.call-update) | async-done | bytes 40976 | tf_op jit(solution)/shard_map/reduce_scatter | solution.py:58
  147.5 0.8 reshape.82
  148.4 2.9 %convert_bitcast_fusion = bf16[20,4,96,96]{2,3,0,1:T(8,128)(2,1)} fusion(f32[20,4,256]{2,0,1:T(8,128)S(1)} %copy.74, f32[4,96,256]{2,1,0:T(8,128)S(1)} %copy.62, bf16[4,96,256,1]{2,0,1,3:T(4,128)(2,1)S(1)} %copy-done.8), kind=kOutput, calls=%fused_computation.24 | convolution fusion | flops 382156800 | bytes 2146304 | tf_op jit(solution)/shard_map/kyqz,yhz->kyqh/dot_general | solution.py:67
  151.2 3.2 %copy.76 = bf16[20,4,96,96]{3,2,1,0:T(8,128)(2,1)S(1)} copy(bf16[20,4,96,96]{2,3,0,1:T(8,128)(2,1)} %convert_bitcast_fusion) | data formatting | bytes 2949120 | tf_op jit(solution)/shard_map/convert_element_type | solution.py:82
  154.4 3.6 %convert_element_type.119 = bf16[80,9216]{1,0:T(8,128)(2,1)} reshape(bf16[20,4,96,96]{3,2,1,0:T(8,128)(2,1)S(1)} %copy.76) | data formatting | bytes 2949120 | tf_op jit(solution)/shard_map/convert_element_type | solution.py:82
  158.0 0.0 all-reduce.5.cloned.1.call-update
  158.0 59.7 %all-reduce.5.cloned.1.call-done = bf16[80,9216]{1,0:T(8,128)(2,1)} async-done(((bf16[80,9216]{1,0:T(8,128)(2,1)}), bf16[80,9216]{1,0:T(8,128)(2,1)}) %all-reduce.5.cloned.1.call-update) | async-done | bytes 1474576 | tf_op jit(solution)/shard_map/psum | solution.py:82
  217.7 4.8 %fusion.12 = bf16[80,9216]{1,0:T(8,128)(2,1)S(1)} fusion(f32[80,9216]{1,0:T(8,128)} %reshape.80, f32[80,9216]{1,0:T(8,128)} %tile.9, bf16[80,9216]{1,0:T(8,128)(2,1)} %all-reduce.5.cloned.1.call-done, bf16[80,9216]{1,0:T(8,128)(2,1)} %all-reduce.3.cloned.1.call-done), kind=kLoop, calls=%fused_computation.20 | loop fusion | flops 11796480 | bytes 10321920 | tf_op jit(solution)/shard_map/convert_element_type | solution.py:79
  222.5 1.4 reshape.79
  (11 shorter events, 0.2 us)
Async XLA Ops:
  6.5 33.8 %copy-start = (bf16[1,512,1024]{2,1,0:T(8,128)(2,1)S(1)}, bf16[1,512,1024]{2,1,0:T(8,128)(2,1)}, u32[]{:S(2)}) copy-start(bf16[1,512,1024]{2,1,0:T(8,128)(2,1)} %param.15) | copy-start | bytes 3145732
  6.5 18.5 %copy-start.1 = (bf16[1,20,4,9216]{3,2,1,0:T(4,128)(2,1)S(1)}, bf16[1,20,4,9216]{3,2,1,0:T(4,128)(2,1)}, u32[]{:S(2)}) copy-start(bf16[1,20,4,9216]{3,2,1,0:T(4,128)(2,1)} %param.9) | copy-start | bytes 4423684
  6.5 43.5 %reduce-scatter.3.cloned.1.call-start = ((), (), s32[]{:S(2)}) async-start(), calls=%async_computation.2 | async-start | bytes 122880 | tf_op jit(solution)/shard_map/reduce_scatter | solution.py:58
  7.4 20.3 %copy-start.5 = (s32[4]{0:T(128)S(1)}, s32[4]{0:T(128)}, u32[]{:S(2)}) copy-start(s32[4]{0:T(128)} %param.11) | copy-start | bytes 52
  28.0 2.9 %copy-start.6 = (bf16[4,96,256,1]{2,0,1,3:T(4,128)(2,1)}, bf16[4,96,256,1]{2,0,1,3:T(4,128)(2,1)S(1)}, u32[]{:S(2)}) copy-start(bf16[4,96,256,1]{2,0,1,3:T(4,128)(2,1)S(1)} %fusion.16) | copy-start | bytes 589828
  40.3 2.9 %copy-start.4 = (s32[1,4,2]{1,2,0:T(2,128)S(1)}, s32[1,4,2]{1,2,0:T(2,128)}, u32[]{:S(2)}) copy-start(s32[1,4,2]{1,2,0:T(2,128)} %param.10) | copy-start | bytes 100
  41.5 9.4 %copy-start.7 = (bf16[4,96,256,1]{2,0,1,3:T(4,128)(2,1)S(1)}, bf16[4,96,256,1]{2,0,1,3:T(4,128)(2,1)}, u32[]{:S(2)}) copy-start(bf16[4,96,256,1]{2,0,1,3:T(4,128)(2,1)} %copy-done.6) | copy-start | bytes 589828
  41.5 78.7 %all-reduce.3.cloned.1.call-start = ((), (), s32[]{:S(2)}) async-start(), calls=%async_computation.3 | async-start | bytes 2949120 | tf_op jit(solution)/shard_map/psum | solution.py:82
  56.9 3.7 %copy-start.2 = (f32[4,96]{1,0:T(4,128)S(1)}, f32[4,96]{1,0:T(4,128)}, u32[]{:S(2)}) copy-start(f32[4,96]{1,0:T(4,128)} %param.13) | copy-start | bytes 4612
  56.9 4.2 %copy-start.3 = (f32[4,96]{1,0:T(4,128)S(1)}, f32[4,96]{1,0:T(4,128)}, u32[]{:S(2)}) copy-start(f32[4,96]{1,0:T(4,128)} %param.14) | copy-start | bytes 4612
  60.5 87.0 %reduce-scatter.5.cloned.1.call-start = ((), (), s32[]{:S(2)}) async-start(), calls=%async_computation.4 | async-start | bytes 122880 | tf_op jit(solution)/shard_map/reduce_scatter | solution.py:58
  124.0 2.9 %copy-start.8 = (bf16[4,96,256,1]{2,0,1,3:T(4,128)(2,1)S(1)}, bf16[4,96,256,1]{2,0,1,3:T(4,128)(2,1)}, u32[]{:S(2)}) copy-start(bf16[4,96,256,1]{2,0,1,3:T(4,128)(2,1)} %copy-done.6) | copy-start | bytes 589828
  139.8 77.8 %all-reduce.5.cloned.1.call-start = ((), (), s32[]{:S(2)}) async-start(), calls=%async_computation.5 | async-start | bytes 2949120 | tf_op jit(solution)/shard_map/psum | solution.py:82
Sparse Core Ops, SparseCore 0:
  41.6 8.3 reduce-scatter.2
  60.7 59.5 all-reduce.2
  140.0 7.5 reduce-scatter.4
  158.1 59.5 all-reduce.4
